TPU v7x, 256 devices: a whole 4x4x8 slice. The times are simulated.
256 devices in a mesh: section: 4 (over y), chan: 64 (over x, z, core).
Axes of the slice: x: 4, y: 4, z: 8, core: 2. Of those that a mesh axis runs over, the one named last changes fastest.
Arguments:
- voltages: bfloat16 [2, 1024, 16, 4096], P(None, 'chan', 'section'), may hold values from -6 to 6
- coefficients: float32 [4, 4096], replicated, may hold values from -0.046875 to 0.046875
- tile_order: int32 [64, 36], P('chan'), may hold values from 0 to 35, each once within a row
- steer_table: bfloat16 [256, 2, 512], replicated, may hold values from -0.1875 to 0.1875
- beam_index: int32 [256, 64], P(None, 'chan'), may hold values from 0 to 255
Outputs:
- visibility: float32 [64, 36, 2, 128, 128], P('chan', 'section')
- beam_power: float32 [2, 256, 16, 4096], P(None, None, 'section', 'chan')
Inputs may be any that keep to these rules, and one draw needn't show every extreme that they name: Row g of tile_order lists each of the 36 work items of channel column g exactly once.
All inputs are finite; a program needn't handle non-finite values.
Results may differ from a plain program's by a relative error of at most 0.0029.
Values may be sent and summed in bfloat16 or wider, within the bound.
A program may use at most 64 MiB of HBM per device.

v0:
```python
import math
import jax
import jax.numpy as jnp
from jax import lax
from jax.sharding import PartitionSpec as P

STATIONS = 512
INPUTS = 1024
NA = 64
NB = 64
AVG = 64
TB = 128
PAIRS = 36
NBEAM = 256


def shifted(value, axis, by):
    devices = lax.axis_size(axis)
    pairs = [(i, i + by) for i in range(devices) if 0 <= i + by < devices]
    return lax.ppermute(value, axis, pairs)


def dft_table(length):
    counter = lax.iota(jnp.int32, length)
    phases = counter[:, None] * counter[None, :] % length
    angles = 2.0 * math.pi / length * phases.astype(jnp.float32)
    cosine = jnp.cos(angles)
    sine_part = jnp.sin(angles)
    return jnp.stack([jnp.stack([cosine, -sine_part]), jnp.stack([sine_part, cosine])])


def channelize(filtered):
    spectra_count = filtered.shape[1]
    length = NA * NB
    blocks = filtered.reshape(2, spectra_count, NA, NB)
    section_one = jnp.einsum("qmab,qrac->rmcb", blocks, dft_table(NA), precision=lax.Precision.HIGH)
    row_index = lax.iota(jnp.int32, NA)
    col_index = lax.iota(jnp.int32, NB)
    angles = (
        2.0
        * math.pi
        / length
        * (row_index[:, None] * col_index[None, :] % length).astype(jnp.float32)
    )
    cosine = jnp.cos(angles)
    sine_part = jnp.sin(angles)
    turned_real = section_one[0] * cosine + section_one[1] * sine_part
    turned_imag = section_one[1] * cosine - section_one[0] * sine_part
    twisted = jnp.stack([turned_real, turned_imag])
    section_two = jnp.einsum(
        "rmcb,rsbd->smdc", twisted, dft_table(NB), precision=lax.Precision.HIGH
    )
    return section_two.reshape(2, spectra_count, length)


def pair_products(spectra, work_items):
    tile_count = INPUTS // TB
    local_channel = work_items // PAIRS
    pair_number = work_items % PAIRS
    tile_ids = lax.iota(jnp.int32, tile_count)
    first_pairs = tile_ids * (tile_ids + 1) // 2
    row_tiles = (
        jnp.sum((first_pairs[None, :] <= pair_number[:, None]).astype(jnp.int32), axis=1) - 1
    )
    col_tiles = pair_number - row_tiles * (row_tiles + 1) // 2
    frame_count = spectra.shape[2]
    channel_groups = spectra.shape[3] // AVG
    blocks = spectra.reshape(2, tile_count, TB, frame_count, channel_groups, AVG)
    tile_table = jnp.transpose(blocks, (1, 4, 0, 2, 3, 5)).reshape(
        tile_count * channel_groups, 2, TB, frame_count * AVG
    )
    row_block = jnp.take(tile_table, row_tiles * channel_groups + local_channel, axis=0)
    col_block = jnp.take(tile_table, col_tiles * channel_groups + local_channel, axis=0)
    swapped = jnp.stack([row_block[:, 1], -row_block[:, 0]], axis=1)
    numbers = (((1, 3), (1, 3)), ((0,), (0,)))
    real_part = lax.dot_general(row_block, col_block, numbers, preferred_element_type=jnp.float32)
    imag_part = lax.dot_general(swapped, col_block, numbers, preferred_element_type=jnp.float32)
    return jnp.stack([real_part, imag_part], axis=1)


def shards(voltages, coefficients, tile_order, steer_table, beam_index):
    section_count = lax.axis_size("section")
    inputs_dev = voltages.shape[1]
    frames_dev = voltages.shape[2]
    tap_count = coefficients.shape[0]
    history = shifted(voltages[:, :, frames_dev - (tap_count - 1) :, :], "section", 1)
    extended = jnp.concatenate([history, voltages], axis=2).astype(jnp.float32)
    filtered = jnp.zeros(voltages.shape, jnp.float32)
    for tap_index in range(tap_count):
        offset = tap_count - 1 - tap_index
        filtered = (
            filtered + coefficients[tap_index] * extended[:, :, offset : offset + frames_dev, :]
        )
    spectra = (
        channelize(filtered.reshape(2, inputs_dev * frames_dev, NA * NB))
        .reshape(voltages.shape)
        .astype(jnp.bfloat16)
    )
    weights = steer_table[beam_index]
    out_dev = beam_index.shape[1]
    shard_piece = lax.all_to_all(spectra, "chan", split_axis=3, concat_axis=1, tiled=True)
    frame_count = shard_piece.shape[2]
    grouped = shard_piece.reshape(2, STATIONS, 2, frame_count, out_dev, AVG)
    product = lax.dot_general(
        weights, grouped, (((3,), (1,)), ((1,), (4,))), preferred_element_type=jnp.float32
    )
    real_part = product[:, :, 0, 0] - product[:, :, 1, 1]
    imag_part = product[:, :, 0, 1] + product[:, :, 1, 0]
    beam_energy = real_part * real_part + imag_part * imag_part
    beam_power = jnp.transpose(beam_energy, (2, 1, 3, 0, 4)).reshape(
        2, NBEAM, frame_count, out_dev * AVG
    )
    column_items = tile_order[0]
    items_dev = column_items.shape[0] // section_count
    mean_factor = 1.0 / (frames_dev * section_count * AVG)
    own_items = lax.dynamic_slice_in_dim(
        column_items, lax.axis_index("section") * items_dev, items_dev
    )
    totals = pair_products(lax.all_gather(shard_piece, "section", axis=2, tiled=True), own_items)
    visibility = (totals * mean_factor)[None]
    return (visibility, beam_power)


def solution(mesh):
    placed = (P(None, "chan", "section", None), P(), P("chan", None), P(), P(None, "chan"))
    return jax.shard_map(
        shards,
        mesh=mesh,
        in_specs=placed,
        out_specs=(P("chan", "section", None, None, None), P(None, None, "section", "chan")),
        check_vma=False,
    )
```

profile of v0, /device:TPU:1, one launch (start us, length us, event | category | flops | bytes accessed | tf_op | source)
XLA Modules:
  0.0 257.8 jit_solution(14299678543089905093)
XLA Ops:
  7.2 0.0 copy-start
  7.2 0.0 copy-start.4
  7.2 0.0 all-gather.2.cloned.1.call-start
  7.2 1.9 slice.54
  9.1 0.0 copy-start.3
  9.2 0.6 copy.79
  9.7 4.1 %collective-permute-start = (bf16[2,16,3,4096]{3,1,2,0:T(8,128)(2,1)S(1)}, bf16[2,16,3,4096]{3,1,2,0:T(8,128)(2,1)S(1)}, u32[]{:S(2)}, u32[]{:S(2)}) collective-permute-start(bf16[2,16,3,4096]{3,1,2,0:T(8,128)(2,1)S(1)} %copy.79), channel_id=1, source_target_pairs={{0,64},{64,128},{128,192},{1,65},{65,129},{129,193},{2,66},{66,130... | collective-permute-start | bytes 2359304 | tf_op jit(solution)/shard_map/ppermute | solution.py:20
  13.8 0.1 fusion.46
  14.0 0.1 fusion.44
  14.1 0.1 fusion.42
  14.3 0.0 copy-done.4
  14.4 15.6 %collective-permute-done = bf16[2,16,3,4096]{3,1,2,0:T(8,128)(2,1)S(1)} collective-permute-done((bf16[2,16,3,4096]{3,1,2,0:T(8,128)(2,1)S(1)}, bf16[2,16,3,4096]{3,1,2,0:T(8,128)(2,1)S(1)}, u32[]{:S(2)}, u32[]{:S(2)}) %collective-permute-start) | collective-permute-done | bytes 786464 | tf_op jit(solution)/shard_map/ppermute | solution.py:20
  30.0 0.7 copy.52
  30.7 0.0 copy-done.3
  30.7 1.0 maximum_convert_fusion
  31.7 1.8 fusion.14
  33.5 3.3 %reshape_reshape.4 = f32[2,64,64,64]{3,2,1,0:T(8,128)} reshape(f32[2,16,4,4096]{3,2,1,0:T(4,128)S(1)} %fusion.14) | data formatting | bytes 4194304 | tf_op jit(solution)/shard_map/reshape;reshape | solution.py:35
  36.9 4.2 %fusion.10 = f32[2,64,64,64]{3,2,1,0:T(8,128)S(1)} fusion(f32[2,64,64,64]{3,2,1,0:T(8,128)} %reshape_reshape.4, f32[1,2,64,64]{2,3,0,1:T(8,128)S(1)} %get-tuple-element.27, f32[1,2,64,64]{2,3,0,1:T(8,128)S(1)} %get-tuple-element.26), kind=kOutput, calls=%fused_computation.18 | convolution fusion | flops 402669568 | bytes 4259840 | tf_op jit(solution)/shard_map/qmab,qrac->rmcb/dot_general | solution.py:36
  41.0 1.0 multiply_add_fusion
  42.0 3.3 %fusion.13 = bf16[2,64,64,64]{3,2,1,0:T(8,128)(2,1)S(1)} fusion(f32[1,2,64,64]{2,3,0,1:T(8,128)S(1)} %get-tuple-element.27, f32[1,2,64,64]{2,3,0,1:T(8,128)S(1)} %get-tuple-element.26, f32[1,64,64,64]{3,2,1,0:T(8,128)S(1)} %get-tuple-element.21, f32[1,64,64,64]{3,2,1,0:T(8,128)S(1)} %get-tuple-element.20), kind=kOutput, calls=%fused_computation.19 | convolution fusion | flops 403718144 | bytes 3211264 | tf_op jit(solution)/shard_map/rmcb,rsbd->smdc/dot_general | solution.py:50
  45.3 2.2 convert_element_type.61
  47.5 12.0 %copy.55 = bf16[2,16,4,4096]{1,2,0,3:T(4,128)(2,1)} copy(bf16[2,16,4,4096]{3,2,1,0:T(4,128)(2,1)} %convert_element_type.61) | data formatting | bytes 2097152 | tf_op jit(solution)/shard_map/convert_element_type | solution.py:97
  59.5 11.9 %reshape.317 = bf16[64,2,4096]{2,1,0:T(2,128)(2,1)S(1)} reshape(bf16[4096,2,4,16]{3,2,1,0:T(4,128)(2,1)} %bitcast.95) | data formatting | bytes 2097152
  71.4 41.3 %all_to_all.18 = bf16[64,2,4096]{2,1,0:T(2,128)(2,1)S(1)} all-to-all(bf16[64,2,4096]{2,1,0:T(2,128)(2,1)S(1)} %reshape.317), channel_id=1, replica_groups=mesh['section'=4,'chan'=64] {'chan'}, dimensions={0} | all-to-all | bytes 2097152 | tf_op jit(solution)/shard_map/all_to_all | solution.py:101
  112.7 7.5 %reshape.318 = bf16[4096,2,4,16]{3,2,1,0:T(4,128)(2,1)} reshape(bf16[64,2,4096]{2,1,0:T(2,128)(2,1)S(1)} %all_to_all.18) | data formatting | bytes 2097152
  120.3 0.0 copy-start.6
  120.3 11.4 %copy.75 = bf16[2,16,4,64,64]{4,1,3,2,0:T(8,128)(2,1)} copy(bf16[2,16,4,64,64]{1,2,0,4,3:T(4,128)(2,1)} %bitcast.94) | data formatting | bytes 2097152 | tf_op jit(solution)/shard_map/all_to_all | solution.py:101
  131.6 0.0 copy-start.5
  131.6 0.0 copy-start.2
  131.6 0.0 all-gather.2.cloned.1.call-update
  131.7 0.0 copy-done.6
  131.7 0.0 copy-done
  131.7 1.7 gather_fusion
  133.5 0.0 copy-done.5
  133.5 0.1 and_select_fusion.1
  133.6 0.1 convert_reduce_fusion
  133.7 0.1 compare_and_fusion.1
  133.8 0.1 compare_and_fusion
  133.9 0.0 copy-done.2
  133.9 3.5 %copy.64 = bf16[2,512,2,4,64]{1,4,3,2,0:T(8,128)(2,1)} copy(bf16[2,512,2,4,64]{4,2,1,3,0:T(2,128)(2,1)S(1)} %bitcast.97) | data formatting | bytes 2097152 | tf_op jit(solution)/shard_map/reshape.8
  137.4 2.0 convolution_bitcast_fusion
  139.4 1.0 fusion.27
  140.3 74.9 %all-gather.2.cloned.1.call-done = bf16[2,1024,16,64]{3,1,2,0:T(8,128)(2,1)} async-done(((bf16[2,1024,4,64]{3,1,2,0:T(8,128)(2,1)}), bf16[2,1024,16,64]{3,1,2,0:T(8,128)(2,1)}) %all-gather.2.cloned.1.call-update) | async-done | bytes 4194320 | tf_op jit(solution)/shard_map/all_gather | solution.py:119
  215.2 8.6 %copy.58 = bf16[2,8,128,16,1,64]{2,5,3,0,1,4:T(8,128)(2,1)} copy(bf16[2,8,128,16,1,64]{5,2,1,3,0,4:T(8,128)(2,1)} %bitcast.98) | data formatting | bytes 8388608 | tf_op jit(solution)/shard_map/reshape | solution.py:68
  223.8 6.5 %copy.59 = bf16[8,2,128,1024]{3,2,1,0:T(8,128)(2,1)} copy(bf16[8,2,128,1024]{2,3,1,0:T(8,128)(2,1)} %bitcast.92) | data formatting | bytes 8388608 | tf_op jit(solution)/shard_map/reshape | solution.py:69
  230.3 5.8 %gather_fusion.2 = bf16[9,2,128,1024]{2,3,1,0:T(8,128)(2,1)} fusion(bf16[8,2,128,1024]{2,3,1,0:T(8,128)(2,1)} %bitcast.93, s32[1024]{0:T(1024)S(1)} %pad_clamp_fusion.1), kind=kCustom, calls=%fused_computation.1.clone | custom fusion | bytes 9437220 | tf_op jit(solution)/shard_map/jit(_take)/gather | solution.py:73
  236.1 5.8 %gather_fusion.1 = bf16[9,2,128,1024]{3,2,1,0:T(8,128)(2,1)} fusion(bf16[8,2,128,1024]{3,2,1,0:T(8,128)(2,1)} %copy.59, s32[1024]{0:T(1024)S(1)} %pad_clamp_fusion.2), kind=kCustom, calls=%fused_computation.clone | custom fusion | bytes 9437220 | tf_op jit(solution)/shard_map/jit(_take)/gather | solution.py:72
  242.0 0.0 slice-start
  242.0 3.0 %broadcast_select_fusion.1 = bf16[9,2,128,1024]{3,2,1,0:T(8,128)(2,1)S(1)} fusion(bf16[9,2,128,1024]{3,2,1,0:T(8,128)(2,1)} %gather_fusion.1, pred[9]{0:T(512)(128)(4,1)S(1)} %get-tuple-element.13), kind=kLoop, calls=%fused_computation.8 | loop fusion | flops 2359296 | bytes 9437193 | tf_op jit(solution)/shard_map/jit(_take)/select_n | solution.py:72
  245.0 0.0 slice-start.1
  245.0 0.3 fusion.54
  245.3 0.3 slice-done
  245.6 0.6 slice-done.1
  246.2 1.5 fusion.20
  247.6 0.0 copy-start.1
  247.6 2.0 fusion.21
  249.7 0.1 maximum_multiply_fusion
  249.8 1.1 copy.65
  250.9 0.0 copy-done.1
  (8 shorter events, 0.1 us)
Async XLA Ops:
  7.2 124.6 %copy-start = (bf16[256,2,512]{2,1,0:T(2,128)(2,1)S(1)}, bf16[256,2,512]{2,1,0:T(2,128)(2,1)}, u32[]{:S(2)}) copy-start(bf16[256,2,512]{2,1,0:T(2,128)(2,1)} %param.10) | copy-start | bytes 1572868
  7.2 7.1 %copy-start.4 = (f32[4,4096]{1,0:T(4,128)S(1)}, f32[4,4096]{1,0:T(4,128)}, u32[]{:S(2)}) copy-start(f32[4,4096]{1,0:T(4,128)} %param.8) | copy-start | bytes 196612
  7.2 208.1 %all-gather.2.cloned.1.call-start = ((), (), s32[]{:S(2)}) async-start(), calls=%async_computation.1 | async-start | bytes 10485760 | tf_op jit(solution)/shard_map/all_gather | solution.py:119
  9.1 21.5 %copy-start.3 = (bf16[2,16,4,4096]{3,2,1,0:T(4,128)(2,1)S(1)}, bf16[2,16,4,4096]{3,2,1,0:T(4,128)(2,1)}, u32[]{:S(2)}) copy-start(bf16[2,16,4,4096]{3,2,1,0:T(4,128)(2,1)} %param.7) | copy-start | bytes 3145732
  9.7 20.2 %collective-permute-start = (bf16[2,16,3,4096]{3,1,2,0:T(8,128)(2,1)S(1)}, bf16[2,16,3,4096]{3,1,2,0:T(8,128)(2,1)S(1)}, u32[]{:S(2)}, u32[]{:S(2)}) collective-permute-start(bf16[2,16,3,4096]{3,1,2,0:T(8,128)(2,1)S(1)} %copy.79), channel_id=1, source_target_pairs={{0,64},{64,128},{128,192},{1,65},{65,129},{129,193},{2,66},{66,130... | collective-permute-start | bytes 2359304 | tf_op jit(solution)/shard_map/ppermute | solution.py:20
  120.3 11.4 %copy-start.6 = (s32[256,1]{0,1:T(1,128)S(1)}, s32[256,1]{0,1:T(1,128)}, u32[]{:S(2)}) copy-start(s32[256,1]{0,1:T(1,128)} %param.11) | copy-start | bytes 3076
  131.6 1.8 copy-start.5
  131.6 2.2 copy-start.2
  242.0 3.6 %slice-start = ((s8[4718592]{0:T(1024)(128)(4,1)}), s8[4194304]{0:T(1024)(128)(4,1)S(1)}, s32[]{:S(2)}) async-start(s8[4718592]{0:T(1024)(128)(4,1)} %bitcast.99), calls=%async_computation.2 | async-start | bytes 8388608
  245.0 1.2 slice-start.1
  247.6 3.3 %copy-start.1 = (bf16[256,2,512]{2,1,0:T(2,128)(2,1)S(1)}, bf16[256,2,512]{2,1,0:T(2,128)(2,1)}, u32[]{:S(2)}) copy-start(bf16[256,2,512]{2,1,0:T(2,128)(2,1)} %param.10) | copy-start | bytes 1572868
Sparse Core Ops, SparseCore 0:
  131.8 83.4 all-gather.1
where the time goes:
time: 259 us; the launch traced here: 258 us
  waiting for transfers between devices  90.6 us (35%)
  local copies, waits for them, and re-layouts  85.5 us (33%)
  blocking collectives  41.3 us (16%)
  between operations  14.3 us (6%)
  matrix products  12.9 us (5%)
  other arithmetic  9 us (3%)
  starting transfers between devices  4.11 us (2%)
    all_gather x1, waiting for transfers between devices, shards(): lax.all_gather(shard_piece, 'section', axis=2, tiled=True)  74.9 us
    all_to_all x1, blocking collectives, shards(): lax.all_to_all(spectra, 'chan', split_axis=3, concat_axis=1, tiled=True)  41.3 us
    unnamed x22, local copies, waits for them, and re-layouts  22.1 us
    ppermute x1, waiting for transfers between devices, shifted(): return lax.ppermute(value, axis, pairs)  15.6 us
    convert_element_type x2, local copies, waits for them, and re-layouts, shards(): spectra = channelize(filtered.reshape(2, inputs_dev * frames_dev, NA * NB...  14.2 us
    all_to_all x1, local copies, waits for them, and re-layouts, shards(): lax.all_to_all(spectra, 'chan', split_axis=3, concat_axis=1, tiled=True)  11.4 us
    reshape x1, local copies, waits for them, and re-layouts, pair_products(): spectra.reshape(2, tile_count, TB, frame_count, channel_groups, AVG)  8.56 us
    reshape x1, local copies, waits for them, and re-layouts, pair_products(): jnp.transpose(blocks, (1, 4, 0, 2, 3, 5))  6.46 us
  transfers between devices with their start and end apart: 2, of which 2 were waited for; matrix products, arithmetic and copies ran while one was open for 4% of the time, Pallas kernels for 0%

commit v1 on v0

--- a/solution.py
+++ b/solution.py
@@ -116,7 +116,13 @@
     own_items = lax.dynamic_slice_in_dim(
         column_items, lax.axis_index("section") * items_dev, items_dev
     )
-    totals = pair_products(lax.all_gather(shard_piece, "section", axis=2, tiled=True), own_items)
+    totals = pair_products(
+        jnp.concatenate(
+            lax.all_to_all(jnp.stack([shard_piece] * lax.axis_size("section")), "section", 0, 0),
+            axis=2,
+        ),
+        own_items,
+    )
     visibility = (totals * mean_factor)[None]
     return (visibility, beam_power)
 

time: 259 us -> 231 us (0.89)
  waiting for transfers between devices: 90.6 us -> 56.8 us
  between operations: 14.3 us -> 0.89 us
  local copies, waits for them, and re-layouts: 85.5 us -> 93.5 us
  starting transfers between devices: 4.11 us -> 9.27 us
  matrix products: 12.9 us -> 16.8 us
    all_gather x1 -> x0, waiting for transfers between devices: 74.9 us -> none  [shards(): lax.all_gather(shard_piece, 'section', axis=2, tiled=True)]
    all_to_all x0 -> x1, waiting for transfers between devices: none -> 41.2 us  [shards(): lax.all_to_all(jnp.stack([shard_piece] * lax.axis_size('section')), 'sect...]
    reshape x1, local copies, waits for them, and re-layouts: 8.56 us -> 2.63 us  [shards(): jnp.concatenate(lax.all_to_all(jnp.stack([shard_piece] * lax.axis_size('s...]
    transpose x0 -> x1, local copies, waits for them, and re-layouts: none -> 5.41 us  [pair_products(): jnp.transpose(blocks, (1, 4, 0, 2, 3, 5))]
    another operation x1 -> x3, local copies, waits for them, and re-layouts: 3.5 us -> 8.86 us  [the longest x2 5.36 us: shards(): jnp.stack([shard_piece] * lax.axis_size('section'))]
    all_to_all x0 -> x1, starting transfers between devices: none -> 5.2 us  [shards(): lax.all_to_all(jnp.stack([shard_piece] * lax.axis_size('section')), 'sect...]
    dot_general x1, matrix products: 1.46 us -> 5.35 us  [pair_products(): lax.dot_general(row_block, col_block, numbers, preferred_element_type=jnp...]
    unnamed x22 -> x23, local copies, waits for them, and re-layouts: 22.1 us -> 25.7 us
where the time goes in v1:
time: 231 us; the launch traced here: 229 us
  local copies, waits for them, and re-layouts  93.5 us (40%)
  waiting for transfers between devices  56.8 us (25%)
  blocking collectives  41.3 us (18%)
  matrix products  16.8 us (7%)
  other arithmetic  10.5 us (5%)
  starting transfers between devices  9.27 us (4%)
    all_to_all x1, blocking collectives, shards(): lax.all_to_all(spectra, 'chan', split_axis=3, concat_axis=1, tiled=True)  41.3 us
    all_to_all x1, waiting for transfers between devices, shards(): lax.all_to_all(jnp.stack([shard_piece] * lax.axis_size('section')), 'sect...  41.2 us
    unnamed x23, local copies, waits for them, and re-layouts  25.7 us
    ppermute x1, waiting for transfers between devices, shifted(): return lax.ppermute(value, axis, pairs)  15.6 us
    convert_element_type x2, local copies, waits for them, and re-layouts, shards(): spectra = channelize(filtered.reshape(2, inputs_dev * frames_dev, NA * NB...  14.1 us
    all_to_all x1, local copies, waits for them, and re-layouts, shards(): lax.all_to_all(spectra, 'chan', split_axis=3, concat_axis=1, tiled=True)  10.6 us
    reshape x1, local copies, waits for them, and re-layouts, pair_products(): jnp.transpose(blocks, (1, 4, 0, 2, 3, 5))  6.72 us
    gather x1, local copies, waits for them, and re-layouts, pair_products(): jnp.take(tile_table, col_tiles * channel_groups + local_channel, axis=0)  5.9 us
  transfers between devices with their start and end apart: 2, of which 2 were waited for; matrix products, arithmetic and copies ran while one was open for 4% of the time, Pallas kernels for 0%

profile of v1, /device:TPU:1, one launch (start us, length us, event | category | flops | bytes accessed | tf_op | source)
XLA Modules:
  0.0 229.0 jit_solution(2958251105458405148)
XLA Ops:
  0.6 0.0 copy-start
  0.6 0.0 copy-start.4
  0.7 0.0 copy-start.6
  0.7 2.0 slice.54
  2.7 0.6 copy.86
  3.2 4.1 %collective-permute-start = (bf16[2,16,3,4096]{3,1,2,0:T(8,128)(2,1)S(1)}, bf16[2,16,3,4096]{3,1,2,0:T(8,128)(2,1)S(1)}, u32[]{:S(2)}, u32[]{:S(2)}) collective-permute-start(bf16[2,16,3,4096]{3,1,2,0:T(8,128)(2,1)S(1)} %copy.86), channel_id=1, source_target_pairs={{0,64},{64,128},{128,192},{1,65},{65,129},{129,193},{2,66},{66,130... | collective-permute-start | bytes 2359304 | tf_op jit(solution)/shard_map/ppermute | solution.py:20
  7.3 0.1 fusion.46
  7.5 0.1 fusion.44
  7.6 0.1 fusion.42
  7.8 0.0 copy-done.6
  7.8 15.6 %collective-permute-done = bf16[2,16,3,4096]{3,1,2,0:T(8,128)(2,1)S(1)} collective-permute-done((bf16[2,16,3,4096]{3,1,2,0:T(8,128)(2,1)S(1)}, bf16[2,16,3,4096]{3,1,2,0:T(8,128)(2,1)S(1)}, u32[]{:S(2)}, u32[]{:S(2)}) %collective-permute-start) | collective-permute-done | bytes 786464 | tf_op jit(solution)/shard_map/ppermute | solution.py:20
  23.5 0.7 copy.56
  24.2 0.0 copy-done.4
  24.2 1.0 maximum_convert_fusion
  25.2 1.8 fusion.14
  27.0 3.4 %reshape_reshape.7 = f32[2,64,64,64]{3,2,1,0:T(8,128)} reshape(f32[2,16,4,4096]{3,2,1,0:T(4,128)S(1)} %fusion.14) | data formatting | bytes 4194304 | tf_op jit(solution)/shard_map/reshape;reshape | solution.py:35
  30.4 4.1 %fusion.10 = f32[2,64,64,64]{3,2,1,0:T(8,128)S(1)} fusion(f32[2,64,64,64]{3,2,1,0:T(8,128)} %reshape_reshape.7, f32[1,2,64,64]{2,3,0,1:T(8,128)S(1)} %get-tuple-element.27, f32[1,2,64,64]{2,3,0,1:T(8,128)S(1)} %get-tuple-element.26), kind=kOutput, calls=%fused_computation.18 | convolution fusion | flops 402669568 | bytes 4259840 | tf_op jit(solution)/shard_map/qmab,qrac->rmcb/dot_general | solution.py:36
  34.5 1.0 multiply_add_fusion
  35.5 3.3 %fusion.13 = bf16[2,64,64,64]{3,2,1,0:T(8,128)(2,1)S(1)} fusion(f32[1,2,64,64]{2,3,0,1:T(8,128)S(1)} %get-tuple-element.27, f32[1,2,64,64]{2,3,0,1:T(8,128)S(1)} %get-tuple-element.26, f32[1,64,64,64]{3,2,1,0:T(8,128)S(1)} %get-tuple-element.21, f32[1,64,64,64]{3,2,1,0:T(8,128)S(1)} %get-tuple-element.20), kind=kOutput, calls=%fused_computation.19 | convolution fusion | flops 403718144 | bytes 3211264 | tf_op jit(solution)/shard_map/rmcb,rsbd->smdc/dot_general | solution.py:50
  38.8 2.2 convert_element_type.61
  41.0 12.0 %copy.59 = bf16[2,16,4,4096]{1,2,0,3:T(4,128)(2,1)} copy(bf16[2,16,4,4096]{3,2,1,0:T(4,128)(2,1)} %convert_element_type.61) | data formatting | bytes 2097152 | tf_op jit(solution)/shard_map/convert_element_type | solution.py:97
  53.0 11.9 %reshape.320 = bf16[64,2,4096]{2,1,0:T(2,128)(2,1)S(1)} reshape(bf16[4096,2,4,16]{3,2,1,0:T(4,128)(2,1)} %bitcast.105) | data formatting | bytes 2097152
  64.9 41.3 %all_to_all.20 = bf16[64,2,4096]{2,1,0:T(2,128)(2,1)S(1)} all-to-all(bf16[64,2,4096]{2,1,0:T(2,128)(2,1)S(1)} %reshape.320), channel_id=1, replica_groups=mesh['section'=4,'chan'=64] {'chan'}, dimensions={0} | all-to-all | bytes 2097152 | tf_op jit(solution)/shard_map/all_to_all | solution.py:101
  106.2 7.6 %reshape.321 = bf16[4096,2,4,16]{3,2,1,0:T(4,128)(2,1)} reshape(bf16[64,2,4096]{2,1,0:T(2,128)(2,1)S(1)} %all_to_all.20) | data formatting | bytes 2097152
  113.8 10.6 %copy.81 = bf16[2,16,4,64,64]{4,1,3,2,0:T(8,128)(2,1)S(1)} copy(bf16[2,16,4,64,64]{1,2,0,4,3:T(4,128)(2,1)} %bitcast.104) | data formatting | bytes 2097152 | tf_op jit(solution)/shard_map/all_to_all | solution.py:101
  124.4 1.6 copy.62
  126.0 3.7 %stack.62 = bf16[4,2,1024,4,64]{2,4,3,1,0:T(8,128)(2,1)} broadcast(bf16[2,1024,4,64]{1,3,2,0:T(8,128)(2,1)} %copy.62), dimensions={1,2,3,4} | broadcast | bytes 5242880 | tf_op jit(solution)/shard_map/stack | solution.py:121
  129.8 0.0 copy-start.8
  129.8 0.0 copy-start.7
  129.8 5.2 %all-to-all-start.1 = ((bf16[4,2,1024,4,64]{2,4,3,1,0:T(8,128)(2,1)}), bf16[4,2,1024,4,64]{2,4,3,1,0:T(8,128)(2,1)}, u32[]{:S(2)}, u32[]{:S(2)}) async-start(bf16[4,2,1024,4,64]{2,4,3,1,0:T(8,128)(2,1)} %stack.62), calls=%async_computation.1 | async-start | bytes 8388608 | tf_op jit(solution)/shard_map/all_to_all | solution.py:121
  135.0 0.0 copy-done.8
  135.0 0.0 copy-done
  135.0 1.7 gather_fusion
  136.8 0.0 copy-done.7
  136.8 0.1 and_select_fusion.1
  136.9 0.1 convert_reduce_fusion
  136.9 0.1 compare_and_fusion.1
  137.0 0.1 compare_and_fusion
  137.2 3.5 %copy.70 = bf16[2,512,2,4,64]{1,4,3,2,0:T(8,128)(2,1)} copy(bf16[2,512,2,4,64]{4,2,1,3,0:T(2,128)(2,1)S(1)} %bitcast.108) | data formatting | bytes 2097152 | tf_op jit(solution)/shard_map/reshape.12
  140.7 2.0 convolution_bitcast_fusion
  142.6 1.0 fusion.27
  143.6 41.2 %all-to-all-done.1 = bf16[4,2,1024,4,64]{2,4,3,1,0:T(8,128)(2,1)} async-done(((bf16[4,2,1024,4,64]{2,4,3,1,0:T(8,128)(2,1)}), bf16[4,2,1024,4,64]{2,4,3,1,0:T(8,128)(2,1)}, u32[]{:S(2)}, u32[]{:S(2)}) %all-to-all-start.1) | async-done | bytes 4194336 | tf_op jit(solution)/shard_map/all_to_all | solution.py:121
  184.7 2.6 %copy.63 = bf16[2,1024,4,4,64]{1,4,3,2,0:T(8,128)(2,1)S(1)} copy(bf16[2,1024,4,4,64]{1,4,3,0,2:T(8,128)(2,1)} %bitcast.26) | data formatting | bytes 8388608 | tf_op jit(solution)/shard_map/reshape | solution.py:120
  187.4 3.1 %copy.87 = bf16[256,8,8,128]{3,2,1,0:T(8,128)(2,1)} copy(bf16[256,8,8,128]{3,1,2,0:T(8,128)(2,1)S(1)} %bitcast.109) | data formatting | bytes 8388608
  190.4 6.7 %copy.65 = bf16[8,2,128,1024]{3,2,1,0:T(8,128)(2,1)} copy(bf16[8,2,128,1024]{2,0,3,1:T(8,128)(2,1)} %bitcast.102) | data formatting | bytes 8388608 | tf_op jit(solution)/shard_map/reshape | solution.py:69
  197.1 5.4 %copy.64 = bf16[8,1,2,128,16,64]{3,5,4,2,0,1:T(8,128)(2,1)} copy(bf16[8,1,2,128,16,64]{3,0,5,4,2,1:T(8,128)(2,1)} %bitcast.103) | data formatting | bytes 8388608 | tf_op jit(solution)/shard_map/transpose | solution.py:69
  202.5 5.8 %gather_fusion.1 = bf16[9,2,128,1024]{3,2,1,0:T(8,128)(2,1)} fusion(bf16[8,2,128,1024]{3,2,1,0:T(8,128)(2,1)} %copy.65, s32[1024]{0:T(1024)S(1)} %pad_clamp_fusion.2), kind=kCustom, calls=%fused_computation.clone | custom fusion | bytes 9437220 | tf_op jit(solution)/shard_map/jit(_take)/gather | solution.py:72
  208.3 2.9 %broadcast_select_fusion.1 = bf16[9,2,128,1024]{3,2,1,0:T(8,128)(2,1)S(1)} fusion(bf16[9,2,128,1024]{3,2,1,0:T(8,128)(2,1)} %gather_fusion.1, pred[9]{0:T(512)(128)(4,1)S(1)} %get-tuple-element.13), kind=kLoop, calls=%fused_computation.8 | loop fusion | flops 2359296 | bytes 9437193 | tf_op jit(solution)/shard_map/jit(_take)/select_n | solution.py:72
  211.2 0.0 copy-start.2
  211.2 1.9 fusion.54
  213.1 0.9 copy-done.2
  214.0 5.9 %gather_fusion.2 = bf16[9,2,128,1024]{2,3,1,0:T(8,128)(2,1)} fusion(bf16[8,2,128,1024]{2,3,1,0:T(8,128)(2,1)} %bitcast.106, s32[1024]{0:T(1024)S(1)} %pad_clamp_fusion.1), kind=kCustom, calls=%fused_computation.1.clone | custom fusion | bytes 9437220 | tf_op jit(solution)/shard_map/jit(_take)/gather | solution.py:73
  219.9 0.0 copy-start.3
  219.9 0.0 copy-start.5
  219.9 5.4 %fusion.20 = f32[1,9,1,128,128]{4,3,1,2,0:T(8,128)S(1)} fusion(bf16[9,2,128,1024]{3,2,1,0:T(8,128)(2,1)} %copy-done.2, bf16[9,2,128,1024]{2,3,1,0:T(8,128)(2,1)} %gather_fusion.2, pred[9]{0:T(512)(128)(4,1)S(1)} %get-tuple-element.16), kind=kOutput, calls=%fused_computation.32 | convolution fusion | flops 606339072 | bytes 10027017 | tf_op jit(solution)/shard_map/dot_general | solution.py:76
  225.3 0.0 copy-done.3
  225.3 0.5 copy-done.5
  225.8 0.0 copy-start.1
  225.8 2.0 fusion.21
  227.8 0.1 maximum_multiply_fusion
  227.9 1.1 copy.71
  229.0 0.0 copy-done.1
  (7 shorter events, 0.1 us)
Async XLA Ops:
  0.6 134.4 %copy-start = (bf16[256,2,512]{2,1,0:T(2,128)(2,1)S(1)}, bf16[256,2,512]{2,1,0:T(2,128)(2,1)}, u32[]{:S(2)}) copy-start(bf16[256,2,512]{2,1,0:T(2,128)(2,1)} %param.10) | copy-start | bytes 1572868
  0.6 23.5 %copy-start.4 = (bf16[2,16,4,4096]{3,2,1,0:T(4,128)(2,1)S(1)}, bf16[2,16,4,4096]{3,2,1,0:T(4,128)(2,1)}, u32[]{:S(2)}) copy-start(bf16[2,16,4,4096]{3,2,1,0:T(4,128)(2,1)} %param.7) | copy-start | bytes 3145732
  0.7 7.1 %copy-start.6 = (f32[4,4096]{1,0:T(4,128)S(1)}, f32[4,4096]{1,0:T(4,128)}, u32[]{:S(2)}) copy-start(f32[4,4096]{1,0:T(4,128)} %param.8) | copy-start | bytes 196612
  3.2 20.2 %collective-permute-start = (bf16[2,16,3,4096]{3,1,2,0:T(8,128)(2,1)S(1)}, bf16[2,16,3,4096]{3,1,2,0:T(8,128)(2,1)S(1)}, u32[]{:S(2)}, u32[]{:S(2)}) collective-permute-start(bf16[2,16,3,4096]{3,1,2,0:T(8,128)(2,1)S(1)} %copy.86), channel_id=1, source_target_pairs={{0,64},{64,128},{128,192},{1,65},{65,129},{129,193},{2,66},{66,130... | collective-permute-start | bytes 2359304 | tf_op jit(solution)/shard_map/ppermute | solution.py:20
  129.8 5.2 %copy-start.8 = (s32[256,1]{0,1:T(1,128)S(1)}, s32[256,1]{0,1:T(1,128)}, u32[]{:S(2)}) copy-start(s32[256,1]{0,1:T(1,128)} %param.11) | copy-start | bytes 3076
  129.8 7.0 %copy-start.7 = (s32[1,36]{1,0:T(1,128)S(1)}, s32[1,36]{1,0:T(1,128)}, u32[]{:S(2)}) copy-start(s32[1,36]{1,0:T(1,128)} %param.9) | copy-start | bytes 436
  129.8 55.0 %all-to-all-start.1 = ((bf16[4,2,1024,4,64]{2,4,3,1,0:T(8,128)(2,1)}), bf16[4,2,1024,4,64]{2,4,3,1,0:T(8,128)(2,1)}, u32[]{:S(2)}, u32[]{:S(2)}) async-start(bf16[4,2,1024,4,64]{2,4,3,1,0:T(8,128)(2,1)} %stack.62), calls=%async_computation.1 | async-start | bytes 8388608 | tf_op jit(solution)/shard_map/all_to_all | solution.py:121
  211.2 2.8 %copy-start.2 = (bf16[9,2,128,1024]{3,2,1,0:T(8,128)(2,1)}, bf16[9,2,128,1024]{3,2,1,0:T(8,128)(2,1)S(1)}, u32[]{:S(2)}) copy-start(bf16[9,2,128,1024]{3,2,1,0:T(8,128)(2,1)S(1)} %broadcast_select_fusion.1) | copy-start | bytes 14155780
  219.9 5.4 %copy-start.3 = (bf16[9,2,128,1024]{2,3,1,0:T(8,128)(2,1)S(1)}, bf16[9,2,128,1024]{2,3,1,0:T(8,128)(2,1)}, u32[]{:S(2)}) copy-start(bf16[9,2,128,1024]{2,3,1,0:T(8,128)(2,1)} %gather_fusion.2) | copy-start | bytes 14155780
  219.9 5.9 %copy-start.5 = (bf16[9,1,128,1024]{3,2,1,0:T(8,128)(2,1)S(1)}, bf16[9,1,128,1024]{3,2,1,0:T(8,128)(2,1)}, u32[]{:S(2)}) copy-start(bf16[9,1,128,1024]{3,2,1,0:T(8,128)(2,1)} %get-tuple-element.19) | copy-start | bytes 7077892
  225.8 3.2 %copy-start.1 = (bf16[256,2,512]{2,1,0:T(2,128)(2,1)S(1)}, bf16[256,2,512]{2,1,0:T(2,128)(2,1)}, u32[]{:S(2)}) copy-start(bf16[256,2,512]{2,1,0:T(2,128)(2,1)} %param.10) | copy-start | bytes 1572868
